TPU v7x, 256 devices: a whole 4x4x8 slice. The times are simulated.
256 devices in a mesh: tm: 16 (over z, core), space: 16 (over y, x).
Axes of the slice: x: 4, y: 4, z: 8, core: 2. Of those that a mesh axis runs over, the one named last changes fastest.
Arguments:
- queries: bfloat16 [16, 2048, 48, 128], P('tm', 'space'), may hold values from -14 to 14
- noisy_keys: bfloat16 [16, 2048, 48, 128], P('tm', 'space'), may hold values from -14 to 14
- noisy_values: bfloat16 [16, 2048, 48, 128], P('tm', 'space'), may hold values from -6 to 6
- cache_keys: bfloat16 [16, 2048, 48, 128], P('tm', 'space'), may hold values from -12 to 12
- cache_values: bfloat16 [16, 2048, 48, 128], P('tm', 'space'), may hold values from -6 to 6
- block_list: int32 [16, 16, 12], P('tm'), may hold values from 0 to 63, as said below
- block_count: int32 [16, 16], P('tm'), may hold values from 1 to 12
- valid_tokens: int32 [16], replicated, may hold values from 1921 to 2048
Outputs:
- attended: bfloat16 [16, 2048, 48, 128], P('tm', 'space')
Inputs may be any that keep to these rules, and one draw needn't show every extreme that they name: `block_list`: entries index the 64 key blocks of stretch c's window in order of offset, the last 16 being stretch c's own blocks. The first block_count[c, a] entries are distinct and name only blocks of stretches 0 or later; the first of them is query block a's own block; later entries repeat that own block.
All inputs are finite; a program needn't handle non-finite values.
Results may differ from a plain program's by a relative error of at most 0.0035.
Values may be sent and summed in bfloat16 or wider, within the bound.
No kernel may reach another device: no remote copies, remote signals or barrier semaphores. Data moves between devices by JAX's collectives and lax.ppermute only.
A program may use at most 128 MiB of HBM per device.

v0:
```python
import math
import jax
import jax.numpy as jnp
from jax import lax
from jax.sharding import PartitionSpec as P

BLOCK = 128
WIN = 4
LIST = 12
NEG = -1e30


def passed_along(block, axis, distance):
    devices = range(lax.axis_size(axis))
    route = [(i - distance, i) for i in devices if i - distance in devices]
    return lax.ppermute(block, axis, route)


def hand_forward(pair):
    earlier = []
    carried = pair
    for distance in range(1, WIN):
        carried = passed_along(carried, "tm", 1)
        earlier.append(carried)
    return earlier


def on_device(
    queries,
    noisy_keys,
    noisy_values,
    cache_keys,
    cache_values,
    block_list,
    block_count,
    valid_tokens,
):
    stretch_now = lax.axis_index("tm")
    fresh = jnp.concatenate((queries, noisy_keys, noisy_values), 0)
    fresh = lax.all_to_all(fresh, "space", split_axis=2, concat_axis=1, tiled=True)
    own_cache = jnp.concatenate((cache_keys, cache_values), 0)
    earlier = hand_forward(own_cache)
    stacked = jnp.stack(earlier[::-1], 0)
    past = lax.all_to_all(stacked, "space", split_axis=3, concat_axis=2, tiled=True)
    stretch_len = fresh.shape[1]
    local_heads = fresh.shape[2]
    head_size = fresh.shape[3]
    block_total = stretch_len // BLOCK
    fresh_heads = jnp.transpose(fresh, (0, 2, 1, 3))
    past_heads = jnp.transpose(past, (1, 3, 0, 2, 4))
    window_keys = jnp.concatenate((past_heads[0], fresh_heads[1][:, None]), 1)
    window_values = jnp.concatenate((past_heads[1], fresh_heads[2][:, None]), 1)
    query_blocks = fresh_heads[0].reshape(local_heads, block_total, BLOCK, head_size)
    key_blocks = window_keys.reshape(local_heads, WIN * block_total, BLOCK, head_size)
    value_blocks = window_values.reshape(local_heads, WIN * block_total, BLOCK, head_size)
    positions = jnp.arange(stretch_len)
    sources = stretch_now - (WIN - 1) + jnp.arange(WIN)
    lengths = valid_tokens[jnp.clip(sources, 0, valid_tokens.shape[0] - 1)]
    key_live = ((sources[:, None] >= 0) & (positions[None, :] < lengths[:, None])).reshape(
        WIN * block_total, BLOCK
    )
    stretch_lists = block_list[0]
    stretch_counts = block_count[0]
    score_scale = 1.0 / math.sqrt(head_size)
    start_best = jnp.full((local_heads, block_total, BLOCK), NEG, jnp.float32)
    start_total = jnp.zeros((local_heads, block_total, BLOCK), jnp.float32)
    start_accum = jnp.zeros((local_heads, block_total, BLOCK, head_size), jnp.float32)

    def slot_step(slot_index, carry):
        row_best, row_total, accum = carry
        chosen = lax.dynamic_slice_in_dim(stretch_lists, slot_index, 1, 1)[:, 0]
        keys_here = key_blocks[:, chosen]
        values_here = value_blocks[:, chosen]
        scores = (
            jnp.einsum(
                "haqd,hakd->haqk", query_blocks, keys_here, preferred_element_type=jnp.float32
            )
            * score_scale
        )
        allowed = (slot_index < stretch_counts)[None, :, None, None] & key_live[chosen][
            None, :, None, :
        ]
        scores = jnp.where(allowed, scores, NEG)
        new_best = jnp.maximum(row_best, jnp.max(scores, axis=-1))
        weights = jnp.where(allowed, jnp.exp(scores - new_best[..., None]), 0.0)
        shrink = jnp.exp(row_best - new_best)
        row_total = row_total * shrink + jnp.sum(weights, axis=-1)
        pieces = jnp.einsum(
            "haqk,hakd->haqd",
            weights.astype(jnp.bfloat16),
            values_here,
            preferred_element_type=jnp.float32,
        )
        accum = accum * shrink[..., None] + pieces
        return (new_best, row_total, accum)

    row_best, row_total, accum = lax.fori_loop(
        0, LIST, slot_step, (start_best, start_total, start_accum)
    )
    mixed_rows = accum / row_total[..., None]
    mixed_rows = mixed_rows.reshape(local_heads, stretch_len, head_size)
    query_live = positions < valid_tokens[stretch_now]
    masked = jnp.where(query_live[None, :, None], mixed_rows, 0.0).astype(jnp.bfloat16)
    attended_local = jnp.transpose(masked, (1, 0, 2))
    return lax.all_to_all(attended_local[None], "space", split_axis=1, concat_axis=2, tiled=True)


def solution(mesh):
    placed = (
        P("tm", "space", None, None),
        P("tm", "space", None, None),
        P("tm", "space", None, None),
        P("tm", "space", None, None),
        P("tm", "space", None, None),
        P("tm", None, None),
        P("tm", None),
        P(),
    )
    return jax.shard_map(
        on_device,
        mesh=mesh,
        in_specs=placed,
        out_specs=P("tm", "space", None, None),
        check_vma=False,
    )
```

profile of v0, /device:TPU:192, one launch (start us, length us, event | category | flops | bytes accessed | tf_op | source)
XLA Modules:
  0.0 597.0 jit_solution(18413690183494990930)
XLA Ops:
  4.9 36.7 %collective-permute-done = bf16[2,128,48,128]{3,1,0,2:T(8,128)(2,1)S(1)} collective-permute-done((bf16[2,128,48,128]{3,1,0,2:T(8,128)(2,1)S(1)}, bf16[2,128,48,128]{3,1,0,2:T(8,128)(2,1)S(1)}, u32[]{:S(2)}, u32[]{:S(2)}) %collective-permute-start) | collective-permute-done | bytes 3145760 | tf_op jit(solution)/shard_map/ppermute | solution.py:16
  47.2 7.1 %all-to-all-start.1 = ((bf16[3,128,48,128]{3,1,0,2:T(8,128)(2,1)}), bf16[3,128,48,128]{3,1,0,2:T(8,128)(2,1)}, u32[]{:S(2)}, u32[]{:S(2)}) async-start(bf16[3,128,48,128]{3,1,0,2:T(8,128)(2,1)} %pad_maximum_fusion.3), calls=%async_computation.1 | async-start | bytes 9437184 | tf_op jit(solution)/shard_map/all_to_all | solution.py:40
  54.3 25.9 %collective-permute-done.1 = bf16[2,128,48,128]{3,1,0,2:T(8,128)(2,1)} collective-permute-done((bf16[2,128,48,128]{3,1,0,2:T(8,128)(2,1)S(1)}, bf16[2,128,48,128]{3,1,0,2:T(8,128)(2,1)}, u32[]{:S(2)}, u32[]{:S(2)}) %collective-permute-start.1) | collective-permute-done | bytes 3145760 | tf_op jit(solution)/shard_map/ppermute | solution.py:16
  82.2 36.9 %collective-permute-done.2 = bf16[2,128,48,128]{3,1,0,2:T(8,128)(2,1)S(1)} collective-permute-done((bf16[2,128,48,128]{3,1,0,2:T(8,128)(2,1)}, bf16[2,128,48,128]{3,1,0,2:T(8,128)(2,1)S(1)}, u32[]{:S(2)}, u32[]{:S(2)}) %collective-permute-start.2) | collective-permute-done | bytes 3145760 | tf_op jit(solution)/shard_map/ppermute | solution.py:16
  119.0 6.3 %pad_maximum_fusion = bf16[3,2,128,48,128]{4,2,1,0,3:T(8,128)(2,1)} fusion(bf16[1,2,128,48,128]{4,2,1,0,3:T(8,128)(2,1)S(1)} %bitcast.98, bf16[1,2,128,48,128]{4,2,1,0,3:T(8,128)(2,1)} %bitcast.5, bf16[1,2,128,48,128]{4,2,1,0,3:T(8,128)(2,1)S(1)} %bitcast.99), kind=kLoop, calls=%fused_computation.37 | loop fusion | flops 9437184 | bytes 18874368 | tf_op jit(solution)/shard_map/stack | solution.py:43
  125.4 3.4 all-to-all-done.1
  128.8 5.0 all-to-all-start
  136.1 3.3 copy.65
  141.3 133.8 %all-to-all-done = bf16[3,2,128,48,128]{4,2,1,0,3:T(8,128)(2,1)} async-done(((bf16[3,2,128,48,128]{4,2,1,0,3:T(8,128)(2,1)}), bf16[3,2,128,48,128]{4,2,1,0,3:T(8,128)(2,1)}, u32[]{:S(2)}, u32[]{:S(2)}) %all-to-all-start) | async-done | bytes 9437216 | tf_op jit(solution)/shard_map/all_to_all | solution.py:44
  275.2 11.6 %copy.60 = bf16[3,2,16,128,3,128]{5,3,2,4,1,0:T(8,128)(2,1)} copy(bf16[3,2,16,128,3,128]{5,3,1,0,4,2:T(8,128)(2,1)} %bitcast.9) | data formatting | bytes 18874368 | tf_op jit(solution)/shard_map/all_to_all | solution.py:44
  286.8 6.6 %slice_bitcast_fusion = (bf16[3,3,2048,128]{3,2,0,1:T(8,128)(2,1)S(1)}, bf16[3,3,2048,128]{3,2,0,1:T(8,128)(2,1)}) fusion(bf16[2,3,3,2048,128]{4,3,1,0,2:T(8,128)(2,1)} %bitcast.91), kind=kLoop, calls=%fused_computation.40 | loop fusion | bytes 18874368 | tf_op jit(solution)/shard_map/squeeze | solution.py:52
  293.4 4.0 pad_maximum_fusion.1
  300.5 3.1 copy.67
  303.6 247.9 %while.18 = (s32[]{:T(128)}, f32[3,16,128]{2,1,0:T(8,128)S(1)}, f32[3,16,128]{2,1,0:T(8,128)S(1)}, f32[3,16,128,128]{3,2,1,0:T(8,128)}, s32[16]{0:T(128)S(1)}, /...) while((s32[]{:T(128)}, f32[3,16,128]{2,1,0:T(8,128)S(1)}, ...), condition=%wide.region_3.4_spmd.clone, body=%wide.region_0.3_spmd.clone.sunk | while | flops 415286336 | bytes 27167672 | solution.py:97
  304.4 4.7 gather_fusion.1
  309.1 4.1 bitcast_reduce_fusion.2
  314.4 4.7 gather_fusion.2
  319.1 4.7 fusion.47
  324.6 4.7 gather_fusion.1
  329.3 4.1 bitcast_reduce_fusion.2
  334.6 4.7 gather_fusion.2
  339.3 5.2 fusion.47
  345.3 4.7 gather_fusion.1
  350.0 4.1 bitcast_reduce_fusion.2
  355.3 4.7 gather_fusion.2
  360.0 5.2 fusion.47
  366.0 4.7 gather_fusion.1
  370.7 4.1 bitcast_reduce_fusion.2
  376.0 4.7 gather_fusion.2
  380.7 5.2 fusion.47
  386.7 4.7 gather_fusion.1
  391.4 4.1 bitcast_reduce_fusion.2
  396.7 4.7 gather_fusion.2
  401.4 5.2 fusion.47
  407.4 4.7 gather_fusion.1
  412.1 4.1 bitcast_reduce_fusion.2
  417.4 4.7 gather_fusion.2
  422.1 5.2 fusion.47
  428.1 4.7 gather_fusion.1
  432.8 4.1 bitcast_reduce_fusion.2
  438.1 4.7 gather_fusion.2
  442.8 5.2 fusion.47
  448.8 4.7 gather_fusion.1
  453.5 4.1 bitcast_reduce_fusion.2
  458.8 4.7 gather_fusion.2
  463.5 5.2 fusion.47
  469.5 4.7 gather_fusion.1
  474.2 4.1 bitcast_reduce_fusion.2
  479.5 4.7 gather_fusion.2
  484.2 5.2 fusion.47
  490.2 4.7 gather_fusion.1
  494.9 4.1 bitcast_reduce_fusion.2
  500.2 4.7 gather_fusion.2
  504.9 5.2 fusion.47
  510.9 4.7 gather_fusion.1
  515.6 4.1 bitcast_reduce_fusion.2
  520.9 4.7 gather_fusion.2
  525.6 5.2 fusion.47
  531.6 4.7 gather_fusion.1
  536.3 4.1 bitcast_reduce_fusion.2
  541.6 4.7 gather_fusion.2
  546.3 5.2 fusion.47
  555.3 7.5 %fusion.23 = bf16[3,2048,128]{2,0,1:T(4,128)(2,1)S(1)} fusion(bf16[3,16,128,128]{3,0,2,1:T(4,128)(2,1)S(1)} %copy.68, pred[2048]{0:T(1024)(128)(4,1)S(1)} %iota_compare_fusion), kind=kLoop, calls=%fused_computation.44 | loop fusion | flops 786432 | bytes 3147776 | tf_op jit(solution)/shard_map/convert_element_type | solution.py:103
  562.8 31.7 %all_to_all.54 = bf16[1,2048,3,128]{3,2,0,1:T(4,128)(2,1)S(1)} all-to-all(bf16[1,2048,3,128]{3,2,0,1:T(4,128)(2,1)S(1)} %bitcast.95), channel_id=1, replica_groups=mesh['tm'=16,'space'=16] {'space'}, dimensions={1} | all-to-all | bytes 3145728 | tf_op jit(solution)/shard_map/all_to_all | solution.py:105
  (166 shorter events, 48.9 us)
Async XLA Ops:
  0.0 1.9 copy-start.1
  2.4 41.1 %copy-start.2 = (bf16[1,128,48,128]{3,2,1,0:T(8,128)(2,1)S(1)}, bf16[1,128,48,128]{3,2,1,0:T(8,128)(2,1)}, u32[]{:S(2)}) copy-start(bf16[1,128,48,128]{3,2,1,0:T(8,128)(2,1)} %param.10) | copy-start | bytes 4718596
  2.7 41.2 %copy-start.3 = (bf16[1,128,48,128]{3,2,1,0:T(8,128)(2,1)S(1)}, bf16[1,128,48,128]{3,2,1,0:T(8,128)(2,1)}, u32[]{:S(2)}) copy-start(bf16[1,128,48,128]{3,2,1,0:T(8,128)(2,1)} %param.11) | copy-start | bytes 4718596
  2.7 41.6 %copy-start.4 = (bf16[1,128,48,128]{3,2,1,0:T(8,128)(2,1)S(1)}, bf16[1,128,48,128]{3,2,1,0:T(8,128)(2,1)}, u32[]{:S(2)}) copy-start(bf16[1,128,48,128]{3,2,1,0:T(8,128)(2,1)} %param.12) | copy-start | bytes 4718596
  2.7 38.9 %collective-permute-start = (bf16[2,128,48,128]{3,1,0,2:T(8,128)(2,1)S(1)}, bf16[2,128,48,128]{3,1,0,2:T(8,128)(2,1)S(1)}, u32[]{:S(2)}, u32[]{:S(2)}) collective-permute-start(bf16[2,128,48,128]{3,1,0,2:T(8,128)(2,1)S(1)} %pad_maximum_fusion.4), channel_id=1, source_target_pairs={{0,16},{16,32},{32,48},{48,64},{64,80},{80,96},{96,112},{112,128},... | collective-permute-start | bytes 9437192 | tf_op jit(solution)/shard_map/ppermute | solution.py:16
  41.6 38.7 %collective-permute-start.1 = (bf16[2,128,48,128]{3,1,0,2:T(8,128)(2,1)S(1)}, bf16[2,128,48,128]{3,1,0,2:T(8,128)(2,1)}, u32[]{:S(2)}, u32[]{:S(2)}) collective-permute-start(bf16[2,128,48,128]{3,1,0,2:T(8,128)(2,1)S(1)} %collective-permute-done), channel_id=1, source_target_pairs={{0,16},{16,32},{32,48},{48,64},{64,80},{80,96},{96,112},{112,128},... | collective-permute-start | bytes 9437192 | tf_op jit(solution)/shard_map/ppermute | solution.py:16
  47.2 81.5 %all-to-all-start.1 = ((bf16[3,128,48,128]{3,1,0,2:T(8,128)(2,1)}), bf16[3,128,48,128]{3,1,0,2:T(8,128)(2,1)}, u32[]{:S(2)}, u32[]{:S(2)}) async-start(bf16[3,128,48,128]{3,1,0,2:T(8,128)(2,1)} %pad_maximum_fusion.3), calls=%async_computation.1 | async-start | bytes 9437184 | tf_op jit(solution)/shard_map/all_to_all | solution.py:40
  80.2 38.8 %collective-permute-start.2 = (bf16[2,128,48,128]{3,1,0,2:T(8,128)(2,1)}, bf16[2,128,48,128]{3,1,0,2:T(8,128)(2,1)S(1)}, u32[]{:S(2)}, u32[]{:S(2)}) collective-permute-start(bf16[2,128,48,128]{3,1,0,2:T(8,128)(2,1)} %collective-permute-done.1), channel_id=1, source_target_pairs={{0,16},{16,32},{32,48},{48,64},{64,80},{80,96},{96,112},{112,128},... | collective-permute-start | bytes 9437192 | tf_op jit(solution)/shard_map/ppermute | solution.py:16
  125.3 8.5 %copy-start = (s32[16]{0:T(128)S(1)}, s32[16]{0:T(128)}, u32[]{:S(2)}) copy-start(s32[16]{0:T(128)} %param.17) | copy-start | bytes 196
  125.3 9.4 %copy-start.5 = (s32[1,16,12]{1,0,2:T(1,128)S(1)}, s32[1,16,12]{1,0,2:T(1,128)}, u32[]{:S(2)}) copy-start(s32[1,16,12]{1,0,2:T(1,128)} %param.15) | copy-start | bytes 2308
  128.8 146.4 %all-to-all-start = ((bf16[3,2,128,48,128]{4,2,1,0,3:T(8,128)(2,1)}), bf16[3,2,128,48,128]{4,2,1,0,3:T(8,128)(2,1)}, u32[]{:S(2)}, u32[]{:S(2)}) async-start(bf16[3,2,128,48,128]{4,2,1,0,3:T(8,128)(2,1)} %pad_maximum_fusion), calls=%async_computation | async-start | bytes 18874368 | tf_op jit(solution)/shard_map/all_to_all | solution.py:44
  300.5 3.1 copy-start.6
where the time goes:
time: 599 us; the launch traced here: 597 us
  waiting for transfers between devices  237 us (40%)
  local copies, waits for them, and re-layouts  159 us (27%)
  matrix products  111 us (19%)
  other arithmetic  39.7 us (7%)
  blocking collectives  31.7 us (5%)
  starting transfers between devices  18.1 us (3%)
    all_to_all x1, waiting for transfers between devices, on_device(): lax.all_to_all(stacked, 'space', split_axis=3, concat_axis=2, tiled=True)  134 us
    ppermute x3, waiting for transfers between devices, passed_along(): return lax.ppermute(block, axis, route)  99.5 us
    dot_general x12, matrix products, slot_step(): jnp.einsum('haqk,hakd->haqd', weights.astype(jnp.bfloat16), values_here,...  62.2 us
    gather x12, local copies, waits for them, and re-layouts, slot_step(): keys_here = key_blocks[:, chosen]  56.5 us
    gather x12, local copies, waits for them, and re-layouts, slot_step(): values_here = value_blocks[:, chosen]  56.5 us
    dot_general x12, matrix products, slot_step(): jnp.einsum('haqd,hakd->haqk', query_blocks, keys_here, preferred_element_...  49.1 us
    all_to_all x1, blocking collectives, on_device(): lax.all_to_all(attended_local[None], 'space', split_axis=1, concat_axis=2...  31.7 us
    reduce_sum x12, other arithmetic, slot_step(): row_total = row_total * shrink + jnp.sum(weights, axis=-1)  13.6 us
  transfers between devices with their start and end apart: 5, of which 5 were waited for; matrix products, arithmetic and copies ran while one was open for 3% of the time, Pallas kernels for 0%

commit v1 on v0

--- a/solution.py
+++ b/solution.py
@@ -102,7 +102,15 @@
     query_live = positions < valid_tokens[stretch_now]
     masked = jnp.where(query_live[None, :, None], mixed_rows, 0.0).astype(jnp.bfloat16)
     attended_local = jnp.transpose(masked, (1, 0, 2))
-    return lax.all_to_all(attended_local[None], "space", split_axis=1, concat_axis=2, tiled=True)
+    return jnp.concatenate(
+        lax.all_to_all(
+            jnp.stack(jnp.split(attended_local[None], lax.axis_size("space"), axis=1)),
+            "space",
+            0,
+            0,
+        ),
+        axis=2,
+    )
 
 
 def solution(mesh):

time: 599 us -> 586 us (0.978)
  other arithmetic: 39.7 us -> 32.9 us
    convert_element_type x1, other arithmetic: 7.49 us -> 0.69 us  [on_device(): jnp.where(query_live[None, :, None], mixed_rows, 0.0).astype(jnp.bfloat16)]
where the time goes in v1:
time: 586 us; the launch traced here: 584 us
  waiting for transfers between devices  237 us (40%)
  local copies, waits for them, and re-layouts  158 us (27%)
  matrix products  111 us (19%)
  other arithmetic  32.9 us (6%)
  blocking collectives  26 us (4%)
  starting transfers between devices  17.9 us (3%)
    all_to_all x1, waiting for transfers between devices, on_device(): lax.all_to_all(stacked, 'space', split_axis=3, concat_axis=2, tiled=True)  134 us
    ppermute x3, waiting for transfers between devices, passed_along(): return lax.ppermute(block, axis, route)  98.5 us
    dot_general x12, matrix products, slot_step(): jnp.einsum('haqk,hakd->haqd', weights.astype(jnp.bfloat16), values_here,...  62.2 us
    gather x12, local copies, waits for them, and re-layouts, slot_step(): keys_here = key_blocks[:, chosen]  56.5 us
    gather x12, local copies, waits for them, and re-layouts, slot_step(): values_here = value_blocks[:, chosen]  56.5 us
    dot_general x12, matrix products, slot_step(): jnp.einsum('haqd,hakd->haqk', query_blocks, keys_here, preferred_element_...  49.1 us
    all_to_all x1, blocking collectives, on_device(): lax.all_to_all(jnp.stack(jnp.split(attended_local[None], lax.axis_size('s...  26 us
    reduce_sum x12, other arithmetic, slot_step(): row_total = row_total * shrink + jnp.sum(weights, axis=-1)  13.6 us
  transfers between devices with their start and end apart: 5, of which 5 were waited for; matrix products, arithmetic and copies ran while one was open for 3% of the time, Pallas kernels for 0%

profile of v1, /device:TPU:192, one launch (start us, length us, event | category | flops | bytes accessed | tf_op | source)
XLA Modules:
  0.0 584.0 jit_solution(6617103241474957194)
XLA Ops:
  4.8 36.7 %collective-permute-done = bf16[2,128,48,128]{3,1,0,2:T(8,128)(2,1)S(1)} collective-permute-done((bf16[2,128,48,128]{3,1,0,2:T(8,128)(2,1)S(1)}, bf16[2,128,48,128]{3,1,0,2:T(8,128)(2,1)S(1)}, u32[]{:S(2)}, u32[]{:S(2)}) %collective-permute-start) | collective-permute-done | bytes 3145760 | tf_op jit(solution)/shard_map/ppermute | solution.py:16
  48.1 7.1 %all-to-all-start.1 = ((bf16[3,128,48,128]{3,1,0,2:T(8,128)(2,1)}), bf16[3,128,48,128]{3,1,0,2:T(8,128)(2,1)}, u32[]{:S(2)}, u32[]{:S(2)}) async-start(bf16[3,128,48,128]{3,1,0,2:T(8,128)(2,1)} %pad_maximum_fusion.3), calls=%async_computation.1 | async-start | bytes 9437184 | tf_op jit(solution)/shard_map/all_to_all | solution.py:40
  55.2 24.9 %collective-permute-done.1 = bf16[2,128,48,128]{3,1,0,2:T(8,128)(2,1)} collective-permute-done((bf16[2,128,48,128]{3,1,0,2:T(8,128)(2,1)S(1)}, bf16[2,128,48,128]{3,1,0,2:T(8,128)(2,1)}, u32[]{:S(2)}, u32[]{:S(2)}) %collective-permute-start.1) | collective-permute-done | bytes 3145760 | tf_op jit(solution)/shard_map/ppermute | solution.py:16
  82.0 36.9 %collective-permute-done.2 = bf16[2,128,48,128]{3,1,0,2:T(8,128)(2,1)S(1)} collective-permute-done((bf16[2,128,48,128]{3,1,0,2:T(8,128)(2,1)}, bf16[2,128,48,128]{3,1,0,2:T(8,128)(2,1)S(1)}, u32[]{:S(2)}, u32[]{:S(2)}) %collective-permute-start.2) | collective-permute-done | bytes 3145760 | tf_op jit(solution)/shard_map/ppermute | solution.py:16
  118.9 6.3 %pad_maximum_fusion = bf16[3,2,128,48,128]{4,2,1,0,3:T(8,128)(2,1)} fusion(bf16[1,2,128,48,128]{4,2,1,0,3:T(8,128)(2,1)S(1)} %bitcast.177, bf16[1,2,128,48,128]{4,2,1,0,3:T(8,128)(2,1)} %bitcast.5, bf16[1,2,128,48,128]{4,2,1,0,3:T(8,128)(2,1)S(1)} %bitcast.178), kind=kLoop, calls=%fused_computation.37 | loop fusion | flops 9437184 | bytes 18874368 | tf_op jit(solution)/shard_map/stack | solution.py:43
  125.2 4.4 all-to-all-done.1
  129.6 5.0 all-to-all-start
  136.9 3.3 copy.123
  142.2 133.8 %all-to-all-done = bf16[3,2,128,48,128]{4,2,1,0,3:T(8,128)(2,1)} async-done(((bf16[3,2,128,48,128]{4,2,1,0,3:T(8,128)(2,1)}), bf16[3,2,128,48,128]{4,2,1,0,3:T(8,128)(2,1)}, u32[]{:S(2)}, u32[]{:S(2)}) %all-to-all-start) | async-done | bytes 9437216 | tf_op jit(solution)/shard_map/all_to_all | solution.py:44
  276.0 11.6 %copy.118 = bf16[3,2,16,128,3,128]{5,3,2,4,1,0:T(8,128)(2,1)} copy(bf16[3,2,16,128,3,128]{5,3,1,0,4,2:T(8,128)(2,1)} %bitcast.9) | data formatting | bytes 18874368 | tf_op jit(solution)/shard_map/all_to_all | solution.py:44
  287.6 6.6 %slice_bitcast_fusion = (bf16[3,3,2048,128]{3,2,0,1:T(8,128)(2,1)S(1)}, bf16[3,3,2048,128]{3,2,0,1:T(8,128)(2,1)}) fusion(bf16[2,3,3,2048,128]{4,3,1,0,2:T(8,128)(2,1)} %bitcast.156), kind=kLoop, calls=%fused_computation.40 | loop fusion | bytes 18874368 | tf_op jit(solution)/shard_map/squeeze | solution.py:52
  294.2 4.0 pad_maximum_fusion.1
  298.3 3.1 copy.124
  301.4 3.1 copy.125
  304.5 247.9 %while.18 = (s32[]{:T(128)}, f32[3,16,128]{2,1,0:T(8,128)S(1)}, f32[3,16,128]{2,1,0:T(8,128)S(1)}, f32[3,16,128,128]{3,2,1,0:T(8,128)}, s32[16]{0:T(128)S(1)}, /...) while((s32[]{:T(128)}, f32[3,16,128]{2,1,0:T(8,128)S(1)}, ...), condition=%wide.region_3.4_spmd.clone, body=%wide.region_0.3_spmd.clone.sunk | while | flops 415286336 | bytes 27167672 | solution.py:97
  305.2 4.7 gather_fusion.1
  309.9 4.1 bitcast_reduce_fusion.2
  315.2 4.7 gather_fusion.2
  319.9 4.7 fusion.63
  325.4 4.7 gather_fusion.1
  330.1 4.1 bitcast_reduce_fusion.2
  335.4 4.7 gather_fusion.2
  340.1 5.2 fusion.63
  346.1 4.7 gather_fusion.1
  350.8 4.1 bitcast_reduce_fusion.2
  356.1 4.7 gather_fusion.2
  360.8 5.2 fusion.63
  366.8 4.7 gather_fusion.1
  371.5 4.1 bitcast_reduce_fusion.2
  376.8 4.7 gather_fusion.2
  381.5 5.2 fusion.63
  387.5 4.7 gather_fusion.1
  392.2 4.1 bitcast_reduce_fusion.2
  397.5 4.7 gather_fusion.2
  402.2 5.2 fusion.63
  408.2 4.7 gather_fusion.1
  412.9 4.1 bitcast_reduce_fusion.2
  418.2 4.7 gather_fusion.2
  422.9 5.2 fusion.63
  428.9 4.7 gather_fusion.1
  433.6 4.1 bitcast_reduce_fusion.2
  438.9 4.7 gather_fusion.2
  443.6 5.2 fusion.63
  449.6 4.7 gather_fusion.1
  454.3 4.1 bitcast_reduce_fusion.2
  459.6 4.7 gather_fusion.2
  464.3 5.2 fusion.63
  470.3 4.7 gather_fusion.1
  475.0 4.1 bitcast_reduce_fusion.2
  480.3 4.7 gather_fusion.2
  485.0 5.2 fusion.63
  491.0 4.7 gather_fusion.1
  495.8 4.1 bitcast_reduce_fusion.2
  501.0 4.7 gather_fusion.2
  505.7 5.2 fusion.63
  511.7 4.7 gather_fusion.1
  516.5 4.1 bitcast_reduce_fusion.2
  521.7 4.7 gather_fusion.2
  526.4 5.2 fusion.63
  532.4 4.7 gather_fusion.1
  537.2 4.1 bitcast_reduce_fusion.2
  542.4 4.7 gather_fusion.2
  547.1 5.2 fusion.63
  555.9 26.0 %all_to_all.41 = bf16[16,1,128,3,128]{4,2,3,1,0:T(8,128)(2,1)S(1)} all-to-all(bf16[16,1,128,3,128]{4,2,3,1,0:T(8,128)(2,1)S(1)} %fusion.24), channel_id=1, replica_groups=mesh['tm'=16,'space'=16] {'space'}, dimensions={0} | all-to-all | bytes 3145728 | tf_op jit(solution)/shard_map/all_to_all | solution.py:106
  (179 shorter events, 45.9 us)
Async XLA Ops:
  0.0 1.9 copy-start.1
  2.4 41.0 %copy-start.2 = (bf16[1,128,48,128]{3,2,1,0:T(8,128)(2,1)S(1)}, bf16[1,128,48,128]{3,2,1,0:T(8,128)(2,1)}, u32[]{:S(2)}) copy-start(bf16[1,128,48,128]{3,2,1,0:T(8,128)(2,1)} %param.10) | copy-start | bytes 4718596
  2.7 41.1 %copy-start.3 = (bf16[1,128,48,128]{3,2,1,0:T(8,128)(2,1)S(1)}, bf16[1,128,48,128]{3,2,1,0:T(8,128)(2,1)}, u32[]{:S(2)}) copy-start(bf16[1,128,48,128]{3,2,1,0:T(8,128)(2,1)} %param.11) | copy-start | bytes 4718596
  2.7 38.7 %collective-permute-start = (bf16[2,128,48,128]{3,1,0,2:T(8,128)(2,1)S(1)}, bf16[2,128,48,128]{3,1,0,2:T(8,128)(2,1)S(1)}, u32[]{:S(2)}, u32[]{:S(2)}) collective-permute-start(bf16[2,128,48,128]{3,1,0,2:T(8,128)(2,1)S(1)} %pad_maximum_fusion.4), channel_id=1, source_target_pairs={{0,16},{16,32},{32,48},{48,64},{64,80},{80,96},{96,112},{112,128},... | collective-permute-start | bytes 9437192 | tf_op jit(solution)/shard_map/ppermute | solution.py:16
  41.4 38.7 %collective-permute-start.1 = (bf16[2,128,48,128]{3,1,0,2:T(8,128)(2,1)S(1)}, bf16[2,128,48,128]{3,1,0,2:T(8,128)(2,1)}, u32[]{:S(2)}, u32[]{:S(2)}) collective-permute-start(bf16[2,128,48,128]{3,1,0,2:T(8,128)(2,1)S(1)} %collective-permute-done), channel_id=1, source_target_pairs={{0,16},{16,32},{32,48},{48,64},{64,80},{80,96},{96,112},{112,128},... | collective-permute-start | bytes 9437192 | tf_op jit(solution)/shard_map/ppermute | solution.py:16
  43.8 1.4 copy-start.4
  48.1 81.5 %all-to-all-start.1 = ((bf16[3,128,48,128]{3,1,0,2:T(8,128)(2,1)}), bf16[3,128,48,128]{3,1,0,2:T(8,128)(2,1)}, u32[]{:S(2)}, u32[]{:S(2)}) async-start(bf16[3,128,48,128]{3,1,0,2:T(8,128)(2,1)} %pad_maximum_fusion.3), calls=%async_computation.1 | async-start | bytes 9437184 | tf_op jit(solution)/shard_map/all_to_all | solution.py:40
  80.1 38.8 %collective-permute-start.2 = (bf16[2,128,48,128]{3,1,0,2:T(8,128)(2,1)}, bf16[2,128,48,128]{3,1,0,2:T(8,128)(2,1)S(1)}, u32[]{:S(2)}, u32[]{:S(2)}) collective-permute-start(bf16[2,128,48,128]{3,1,0,2:T(8,128)(2,1)} %collective-permute-done.1), channel_id=1, source_target_pairs={{0,16},{16,32},{32,48},{48,64},{64,80},{80,96},{96,112},{112,128},... | collective-permute-start | bytes 9437192 | tf_op jit(solution)/shard_map/ppermute | solution.py:16
  125.2 9.4 %copy-start = (s32[16]{0:T(128)S(1)}, s32[16]{0:T(128)}, u32[]{:S(2)}) copy-start(s32[16]{0:T(128)} %param.17) | copy-start | bytes 196
  125.2 10.4 %copy-start.5 = (s32[1,16,12]{1,0,2:T(1,128)S(1)}, s32[1,16,12]{1,0,2:T(1,128)}, u32[]{:S(2)}) copy-start(s32[1,16,12]{1,0,2:T(1,128)} %param.15) | copy-start | bytes 2308
  129.6 146.4 %all-to-all-start = ((bf16[3,2,128,48,128]{4,2,1,0,3:T(8,128)(2,1)}), bf16[3,2,128,48,128]{4,2,1,0,3:T(8,128)(2,1)}, u32[]{:S(2)}, u32[]{:S(2)}) async-start(bf16[3,2,128,48,128]{4,2,1,0,3:T(8,128)(2,1)} %pad_maximum_fusion), calls=%async_computation | async-start | bytes 18874368 | tf_op jit(solution)/shard_map/all_to_all | solution.py:44
  301.4 3.1 copy-start.6
